TPU v7x, 512 devices: a whole 4x4x16 slice. The times are simulated.
512 devices in a mesh: seq: 64 (over z, y), head: 8 (over x, core).
Axes of the slice: x: 4, y: 4, z: 16, core: 2. Of those that a mesh axis runs over, the one named last changes fastest.
Arguments:
- queries: bfloat16 [32768, 8, 512], P('seq', 'head'), may hold values from -8 to 8
- token_keys: bfloat16 [32768, 8, 512], P('seq', 'head'), may hold values from -8 to 8
- token_values: bfloat16 [32768, 8, 512], P('seq', 'head'), may hold values from -8 to 8
- fast_weights: bfloat16 [512, 8, 3, 512], P(None, 'head'), may hold values from -0.25 to 0.25
- learn_rate: float32 [8], P('head'), may hold values from 1 to 10
- out_gain: float32 [8, 512], P('head'), may hold values from 0.5 to 1.5
- group_lengths: int32 [2], replicated, may hold values from 1 to 24576, 32768 in all
- slot_order: int32 [32768], P('seq'), may hold values from 0 to 32767, as said below
Outputs:
- balanced_out: bfloat16 [32768, 8, 512], P('seq', 'head')
Inputs may be any that keep to these rules, and one draw needn't show every extreme that they name: slot_order is a permutation of the positions; slot j, with r = j % 512, holds a position of the block [e * 512, (e + 1) * 512) with e = r // 8. `group_lengths`: the two lengths sum to 32768; each lies between 8192 and 24576.
All inputs are finite; a program needn't handle non-finite values.
Results may differ from a plain program's by a relative error of at most 0.0075.
Values may be sent and summed in bfloat16 or wider, within the bound.
A program may use at most 64 MiB of HBM per device.

v0:
```python
import math

import jax
import jax.numpy as jnp
from jax import lax
from jax.sharding import PartitionSpec as P

WINDOW = 2048


eps = 1e-06


def shifted(value, axis, steps):
    count = lax.axis_size(axis)
    first, last = (max(0, -steps), min(count, count - steps))
    return lax.ppermute(value, axis, [(source, source + steps) for source in range(first, last)])


def window_attention(queries, token_keys, token_values):
    tok_rows, head_count, head_width = queries.shape
    device_pos = lax.axis_index("seq")
    shifts = (WINDOW + tok_rows - 1) // tok_rows
    own_rows = jnp.stack([token_keys, token_values])
    pieces = []
    for distance in range(shifts, 0, -1):
        pieces.append(shifted(own_rows, "seq", distance))
    pieces.append(own_rows)
    key_slab = jnp.concatenate(pieces, axis=1)
    block_rows = min(tok_rows, 512)
    key_span = WINDOW + block_rows
    score_scale = 1.0 / math.sqrt(head_width)

    def attend(block_index):
        first_row = block_index * block_rows
        scores = (
            jnp.einsum("qhd,khd->hqk", queries, key_slab[0], preferred_element_type=jnp.float32)
            * score_scale
        )
        query_pos = first_row + jnp.arange(block_rows, dtype=jnp.int32)[:, None]
        key_pos = first_row - WINDOW + jnp.arange(key_span, dtype=jnp.int32)[None, :]
        allowed = (
            (key_pos <= query_pos)
            & (key_pos > query_pos - WINDOW)
            & (device_pos * tok_rows + key_pos >= 0)
        )
        scores = jnp.where(allowed[None], scores, -jnp.inf)
        row_max = jnp.max(scores, axis=-1, keepdims=True)
        expo = jnp.exp(scores - row_max)
        prob_rows = (expo / jnp.sum(expo, axis=-1, keepdims=True)).astype(jnp.bfloat16)
        return jnp.einsum(
            "hqk,khd->qhd", prob_rows, key_slab[1], preferred_element_type=jnp.float32
        ).astype(jnp.bfloat16)

    blocks = lax.map(attend, jnp.arange(tok_rows // block_rows, dtype=jnp.int32))
    return blocks.reshape(tok_rows, head_count, head_width)


def swiglu_apply(inputs, weights):
    both_pre = jnp.einsum(
        "thd,fhcd->thcf", inputs, weights[:, :, 0:2, :], preferred_element_type=jnp.float32
    )
    hidden_act = (jax.nn.silu(both_pre[:, :, 0, :]) * both_pre[:, :, 1, :]).astype(jnp.bfloat16)
    return jnp.einsum(
        "thf,fhd->thd", hidden_act, weights[:, :, 2, :], preferred_element_type=jnp.float32
    ).astype(jnp.bfloat16)


def renormed(old_rows, summed, learn_rate, group_count):
    previous = old_rows.astype(jnp.float32)
    updated = previous + learn_rate[None, :, None, None] / group_count * summed
    old_norm = jnp.sqrt(jnp.sum(previous * previous, axis=-1, keepdims=True) + eps)
    new_norm = jnp.sqrt(jnp.sum(updated * updated, axis=-1, keepdims=True) + eps)
    return (updated * (old_norm / new_norm)).astype(jnp.bfloat16)


def fast_section(queries, token_keys, token_values, positions, fast_weights, learn_rate, first_len):
    member = positions < first_len
    group_count = first_len.astype(jnp.float32)
    both_pre = jnp.einsum(
        "thd,fhcd->thcf", token_keys, fast_weights[:, :, 0:2, :], preferred_element_type=jnp.float32
    )
    gate_pre = both_pre[:, :, 0, :]
    up_pre = both_pre[:, :, 1, :]
    sig_gate = jax.nn.sigmoid(gate_pre)
    activation = (jax.nn.silu(gate_pre) * up_pre).astype(jnp.bfloat16)
    masked_values = jnp.where(member[:, None, None], token_values, jnp.zeros_like(token_values))
    back_act = jnp.einsum(
        "thd,fhd->thf", masked_values, fast_weights[:, :, 2, :], preferred_element_type=jnp.float32
    )
    grad_up = (back_act * gate_pre * sig_gate).astype(jnp.bfloat16)
    grad_gate = (back_act * up_pre * sig_gate * (1.0 + gate_pre * (1.0 - sig_gate))).astype(
        jnp.bfloat16
    )
    term_gate = jnp.einsum(
        "thf,thd->fhd", grad_gate, token_keys, preferred_element_type=jnp.float32
    )
    term_up = jnp.einsum("thf,thd->fhd", grad_up, token_keys, preferred_element_type=jnp.float32)
    term_down = jnp.einsum(
        "thf,thd->fhd", activation, masked_values, preferred_element_type=jnp.float32
    )
    summed = lax.psum(jnp.stack([term_gate, term_up, term_down], axis=2), "seq")
    new_weights = renormed(fast_weights, summed, learn_rate, group_count)
    first_out = swiglu_apply(queries, fast_weights)
    second_out = swiglu_apply(queries, new_weights)
    return jnp.where(member[:, None, None], first_out, second_out)


def token_norm(attention, fast_out, out_gain):
    summed_rows = attention.astype(jnp.float32) + fast_out.astype(jnp.float32)
    local_power = jnp.sum(summed_rows * summed_rows, axis=(1, 2))
    power = lax.psum(local_power, "head")
    total_width = summed_rows.shape[1] * summed_rows.shape[2] * lax.axis_size("head")
    row_scale = lax.rsqrt(power / total_width + eps)
    return (summed_rows * row_scale[:, None, None] * out_gain[None, :, :]).astype(jnp.bfloat16)


def gather_local(source, asked_rows):
    flat_rows = jnp.take(source, asked_rows.reshape(-1), axis=0)
    return flat_rows.reshape(asked_rows.shape + source.shape[1:])


def per_device(
    queries, token_keys, token_values, fast_weights, learn_rate, out_gain, group_lengths, slot_order
):
    tok_rows = queries.shape[0]
    seq_count = lax.axis_size("seq")
    seg_rows = tok_rows // seq_count
    first_len = group_lengths[0]
    attention = window_attention(queries, token_keys, token_values)
    source_dev = jnp.arange(tok_rows, dtype=jnp.int32) // seg_rows
    wanted = (slot_order - source_dev * tok_rows).reshape(seq_count, seg_rows)
    asked_rows = lax.all_to_all(wanted, "seq", split_axis=0, concat_axis=0, tiled=True)
    positions = lax.axis_index("seq") * tok_rows + jnp.arange(tok_rows, dtype=jnp.int32)
    fast_out = fast_section(
        queries, token_keys, token_values, positions, fast_weights, learn_rate, first_len
    )
    normed = token_norm(attention, fast_out, out_gain)
    mixed_here = lax.all_to_all(
        gather_local(normed, asked_rows), "seq", split_axis=0, concat_axis=0, tiled=True
    )
    return mixed_here.reshape(normed.shape)


def solution(mesh):
    return jax.shard_map(
        per_device,
        mesh=mesh,
        in_specs=(
            P("seq", "head", None),
            P("seq", "head", None),
            P("seq", "head", None),
            P(None, "head", None, None),
            P("head"),
            P("head", None),
            P(),
            P("seq"),
        ),
        out_specs=P("seq", "head", None),
        check_vma=False,
    )
```

profile of v0, /device:TPU:1, one launch (start us, length us, event | category | flops | bytes accessed | tf_op | source)
XLA Modules:
  0.0 399.6 jit_solution(7217502497618214827)
XLA Ops:
  6.5 0.0 all-reduce.2.cloned.1.call-start
  6.6 2.4 pad_maximum_fusion.1
  9.0 5.5 %collective-permute-start = (bf16[2,512,1,512]{3,1,2,0:T(8,128)(2,1)}, bf16[2,512,1,512]{3,1,2,0:T(8,128)(2,1)}, u32[]{:S(2)}, u32[]{:S(2)}) collective-permute-start(bf16[2,512,1,512]{3,1,2,0:T(8,128)(2,1)} %pad_maximum_fusion.1), channel_id=1, source_target_pairs={{0,32},{8,40},{16,48},{24,56},{32,64},{40,72},{48,80},{56,88},{64,... | collective-permute-start | bytes 3145736 | tf_op jit(solution)/shard_map/ppermute | solution.py:17
  14.5 5.6 %collective-permute-start.1 = (bf16[2,512,1,512]{3,1,2,0:T(8,128)(2,1)}, bf16[2,512,1,512]{3,1,2,0:T(8,128)(2,1)}, u32[]{:S(2)}, u32[]{:S(2)}) collective-permute-start(bf16[2,512,1,512]{3,1,2,0:T(8,128)(2,1)} %pad_maximum_fusion.1), channel_id=1, source_target_pairs={{0,24},{8,32},{16,40},{24,48},{32,56},{40,64},{48,72},{56,80},{64,... | collective-permute-start | bytes 3145736 | tf_op jit(solution)/shard_map/ppermute | solution.py:17
  20.1 3.6 collective-permute-start.2
  23.8 2.6 collective-permute-start.3
  26.3 3.4 convolution_bitcast_fusion.1
  29.8 0.5 convolution_bitcast_fusion.6
  30.4 1.8 convolution_bitcast_fusion.4
  32.2 0.1 copy-done.5
  32.3 0.6 convolution_bitcast_fusion.5
  32.9 0.5 convolution_bitcast_fusion.3
  33.4 1.9 pad_maximum_fusion
  35.4 0.0 all-reduce.2.cloned.1.call-update
  35.4 0.7 copy-done.10
  36.1 0.7 all_to_all.9
  36.7 14.4 %all-to-all-start = ((s32[64,1,8]{2,1,0:T(1,128)}), s32[64,1,8]{2,1,0:T(1,128)S(1)}, u32[]{:S(2)}, u32[]{:S(2)}) async-start(s32[64,1,8]{2,1,0:T(1,128)} %bitcast), calls=%async_computation | async-start | bytes 65536 | tf_op jit(solution)/shard_map/all_to_all | solution.py:133
  51.2 0.7 convolution_bitcast_fusion.2
  51.9 1.4 fusion.9
  54.1 91.3 %all-to-all-done = s32[64,1,8]{2,1,0:T(1,128)S(1)} async-done(((s32[64,1,8]{2,1,0:T(1,128)}), s32[64,1,8]{2,1,0:T(1,128)S(1)}, u32[]{:S(2)}, u32[]{:S(2)}) %all-to-all-start) | async-done | bytes 2080 | tf_op jit(solution)/shard_map/all_to_all | solution.py:133
  145.4 0.5 broadcast.218
  145.9 0.6 reduce.10
  146.5 0.1 reshape.314
  146.7 1.3 constant_dynamic-update-slice_fusion.4
  148.0 1.3 constant_dynamic-update-slice_fusion.3
  149.3 1.3 constant_dynamic-update-slice_fusion.2
  150.6 1.3 constant_dynamic-update-slice_fusion.1
  151.9 0.1 constant_dynamic-update-slice_fusion
  152.0 2.6 fusion.62
  154.6 2.3 copy-done.3
  157.0 0.8 fusion.2
  157.7 161.7 %all-reduce.2.cloned.1.call-done = f32[512,1,3,512]{3,0,2,1:T(8,128)} async-done(((f32[512,1,3,512]{3,0,2,1:T(8,128)}), f32[512,1,3,512]{3,0,2,1:T(8,128)}) %all-reduce.2.cloned.1.call-update) | async-done | bytes 3145744 | tf_op jit(solution)/shard_map/psum | solution.py:102
  319.4 2.8 fusion.3
  322.3 0.0 copy-start.12
  322.3 0.5 multiply_convert_fusion
  322.8 0.7 convolution_bitcast_fusion
  323.6 0.6 fusion.12
  324.2 0.8 slice-done
  325.0 0.4 slice-done.1
  325.4 1.6 copy-done.8
  327.0 1.6 multiply_reduce_fusion.1
  328.7 20.6 %psum.15 = f32[512]{0:T(512)S(1)} all-reduce(f32[512]{0:T(512)S(1)} %get-tuple-element.24), channel_id=1, replica_groups=mesh['seq'=64,'head'=8] {'head'}, use_global_device_ids=true, to_apply=%region_6.7 | all-reduce | flops 512 | bytes 4096 | tf_op jit(solution)/shard_map/psum | solution.py:112
  349.3 0.2 fusion.28
  349.4 0.2 copy.18
  349.6 2.0 gather_fusion
  351.6 0.1 bitcast_select_fusion.1
  351.8 40.2 %all_to_all.14 = bf16[64,8,1,512]{3,1,2,0:T(8,128)(2,1)S(1)} all-to-all(bf16[64,8,1,512]{3,1,2,0:T(8,128)(2,1)S(1)} %bitcast_select_fusion.1), channel_id=1, replica_groups=mesh['seq'=64,'head'=8] {'seq'}, dimensions={0} | all-to-all | bytes 1048576 | tf_op jit(solution)/shard_map/all_to_all | solution.py:139
  391.9 0.8 copy.29
  (38 shorter events, 0.2 us)
Async XLA Ops:
  6.5 44.6 %copy-start = (bf16[512,1,512]{2,0,1:T(8,128)(2,1)S(1)}, bf16[512,1,512]{2,0,1:T(8,128)(2,1)}, u32[]{:S(2)}) copy-start(bf16[512,1,512]{2,0,1:T(8,128)(2,1)} %param.8) | copy-start | bytes 1572868
  6.5 23.3 %copy-start.6 = (bf16[512,1,512]{2,0,1:T(8,128)(2,1)S(1)}, bf16[512,1,512]{2,0,1:T(8,128)(2,1)}, u32[]{:S(2)}) copy-start(bf16[512,1,512]{2,0,1:T(8,128)(2,1)} %param.10) | copy-start | bytes 1572868
  6.5 23.3 %copy-start.1 = (bf16[512,1,3,512]{3,0,2,1:T(8,128)(2,1)S(1)}, bf16[512,1,3,512]{3,0,2,1:T(8,128)(2,1)}, u32[]{:S(2)}) copy-start(bf16[512,1,3,512]{3,0,2,1:T(8,128)(2,1)} %param.11) | copy-start | bytes 4718596
  6.5 23.2 %copy-start.11 = (s32[2]{0:T(128)S(1)}, s32[2]{0:T(128)}, u32[]{:S(2)}) copy-start(s32[2]{0:T(128)} %param.14) | copy-start | bytes 28
  6.5 312.9 %all-reduce.2.cloned.1.call-start = ((), (), s32[]{:S(2)}) async-start(), calls=%async_computation.2 | async-start | bytes 6291456 | tf_op jit(solution)/shard_map/psum | solution.py:102
  9.0 21.4 %copy-start.4 = (bf16[512,1,512]{2,0,1:T(8,128)(2,1)S(1)}, bf16[512,1,512]{2,0,1:T(8,128)(2,1)}, u32[]{:S(2)}) copy-start(bf16[512,1,512]{2,0,1:T(8,128)(2,1)} %param.9) | copy-start | bytes 1572868
  9.0 137.6 %collective-permute-start = (bf16[2,512,1,512]{3,1,2,0:T(8,128)(2,1)}, bf16[2,512,1,512]{3,1,2,0:T(8,128)(2,1)}, u32[]{:S(2)}, u32[]{:S(2)}) collective-permute-start(bf16[2,512,1,512]{3,1,2,0:T(8,128)(2,1)} %pad_maximum_fusion.1), channel_id=1, source_target_pairs={{0,32},{8,40},{16,48},{24,56},{32,64},{40,72},{48,80},{56,88},{64,... | collective-permute-start | bytes 3145736 | tf_op jit(solution)/shard_map/ppermute | solution.py:17
  14.5 133.5 %collective-permute-start.1 = (bf16[2,512,1,512]{3,1,2,0:T(8,128)(2,1)}, bf16[2,512,1,512]{3,1,2,0:T(8,128)(2,1)}, u32[]{:S(2)}, u32[]{:S(2)}) collective-permute-start(bf16[2,512,1,512]{3,1,2,0:T(8,128)(2,1)} %pad_maximum_fusion.1), channel_id=1, source_target_pairs={{0,24},{8,32},{16,40},{24,48},{32,56},{40,64},{48,72},{56,80},{64,... | collective-permute-start | bytes 3145736 | tf_op jit(solution)/shard_map/ppermute | solution.py:17
  20.1 129.2 %collective-permute-start.2 = (bf16[2,512,1,512]{3,1,2,0:T(8,128)(2,1)}, bf16[2,512,1,512]{3,1,2,0:T(8,128)(2,1)}, u32[]{:S(2)}, u32[]{:S(2)}) collective-permute-start(bf16[2,512,1,512]{3,1,2,0:T(8,128)(2,1)} %pad_maximum_fusion.1), channel_id=1, source_target_pairs={{0,16},{8,24},{16,32},{24,40},{32,48},{40,56},{48,64},{56,72},{64,... | collective-permute-start | bytes 3145736 | tf_op jit(solution)/shard_map/ppermute | solution.py:17
  23.8 126.8 %collective-permute-start.3 = (bf16[2,512,1,512]{3,1,2,0:T(8,128)(2,1)}, bf16[2,512,1,512]{3,1,2,0:T(8,128)(2,1)}, u32[]{:S(2)}, u32[]{:S(2)}) collective-permute-start(bf16[2,512,1,512]{3,1,2,0:T(8,128)(2,1)} %pad_maximum_fusion.1), channel_id=1, source_target_pairs={{0,8},{8,16},{16,24},{24,32},{32,40},{40,48},{48,56},{56,64},{64,7... | collective-permute-start | bytes 3145736 | tf_op jit(solution)/shard_map/ppermute | solution.py:17
  30.4 1.9 copy-start.5
  35.4 0.7 copy-start.10
  36.7 108.6 %all-to-all-start = ((s32[64,1,8]{2,1,0:T(1,128)}), s32[64,1,8]{2,1,0:T(1,128)S(1)}, u32[]{:S(2)}, u32[]{:S(2)}) async-start(s32[64,1,8]{2,1,0:T(1,128)} %bitcast), calls=%async_computation | async-start | bytes 65536 | tf_op jit(solution)/shard_map/all_to_all | solution.py:133
  152.0 2.6 copy-start.7
  154.6 2.3 copy-start.3
  319.4 2.9 copy-start.2
  322.3 1.2 copy-start.12
  322.8 2.2 slice-start
  323.5 1.9 slice-start.1
  323.6 3.5 copy-start.8
  327.0 22.2 %copy-start.9 = (f32[1,512]{1,0:T(1,128)S(1)}, f32[1,512]{1,0:T(1,128)}, u32[]{:S(2)}) copy-start(f32[1,512]{1,0:T(1,128)} %param.13) | copy-start | bytes 6148
Sparse Core Ops, SparseCore 0:
  35.5 283.8 all-reduce.1
where the time goes:
time: 401 us; the launch traced here: 400 us
  waiting for transfers between devices  253 us (63%)
  blocking collectives  60.8 us (15%)
  starting transfers between devices  31.8 us (8%)
  local copies, waits for them, and re-layouts  15.4 us (4%)
  matrix products  14.6 us (4%)
  between operations  14.4 us (4%)
  other arithmetic  9.57 us (2%)
    psum x1, waiting for transfers between devices, fast_section(): summed = lax.psum(jnp.stack([term_gate, term_up, term_down], axis=2), 'seq')  162 us
    all_to_all x1, waiting for transfers between devices, per_device(): lax.all_to_all(wanted, 'seq', split_axis=0, concat_axis=0, tiled=True)  91.3 us
    all_to_all x1, blocking collectives, per_device(): lax.all_to_all(gather_local(normed, asked_rows), 'seq', split_axis=0, con...  40.2 us
    psum x1, blocking collectives, token_norm(): power = lax.psum(local_power, 'head')  20.6 us
    ppermute x4, starting transfers between devices, shifted(): lax.ppermute(value, axis, [(source, source + steps) for source in range(f...  17.3 us
    all_to_all x1, starting transfers between devices, per_device(): lax.all_to_all(wanted, 'seq', split_axis=0, concat_axis=0, tiled=True)  14.4 us
    unnamed x35, local copies, waits for them, and re-layouts  12 us
  transfers between devices with their start and end apart: 6, of which 2 were waited for; matrix products, arithmetic and copies ran while one was open for 5% of the time, Pallas kernels for 0%

commit v1 on v0

v1 whole, which is shorter than its diff:
```python
import functools
import math

import jax
import jax.numpy as jnp
from jax import lax
from jax.experimental import pallas as pl
from jax.experimental.pallas import tpu as pltpu
from jax.sharding import PartitionSpec as P

WINDOW = 2048
CHUNKS = 8
eps = 1e-06
MESH = pl.DeviceIdType.MESH
f32 = jnp.float32
bf16 = jnp.bfloat16


def dot_t(a, b):
    return lax.dot_general(a, b, (((1,), (1,)), ((), ())), preferred_element_type=f32)


def dot_n(a, b):
    return jnp.dot(a, b, preferred_element_type=f32)


def layer_kernel(
    Y, Z, H, UP, DOWN, WIN,
    q_hbm, k_hbm, v_hbm, w_hbm, lr_ref, gain_ref, len_ref, slot_ref,
    out_ref,
    q, kv, w, relay, grad, rs_send_p, rs_send_m, rs_recv_p, rs_recv_m,
    total, y_send, y_recv, new_w, acc, row_m, row_l, first_out, rows,
    power, wanted, asked, send_rows,
    load_sem, win_send, win_recv, relay_send, relay_recv, fwd_send, mid_recv,
    rsp_send, rsp_recv, rsm_send, rsm_recv, ys_send, ys_recv,
    agp_send, agp_recv, agm_send, agm_recv,
    pow_send, pow_recv, idx_send, idx_recv, a2a_send, a2a_recv, own_sem,
):
    T, D = q.shape
    F = w.shape[1]
    FR = F // Z
    N = Y * Z
    SEG = T // N
    CR = T // CHUNKS
    s = lax.axis_index("seq")
    h = lax.axis_index("head")
    z = s // Y
    y = s % Y

    def seq_at(zz, yy):
        return lax.rem(zz + Z, Z) * Y + lax.rem(yy + Y, Y)

    up = seq_at(z + 1, y)
    down = seq_at(z - 1, y)

    def remote(src, dst, ssem, rsem, seq):
        return pltpu.make_async_remote_copy(
            src_ref=src, dst_ref=dst, send_sem=ssem, recv_sem=rsem,
            device_id={"seq": seq}, device_id_type=MESH,
        )

    loads = [
        pltpu.make_async_copy(k_hbm, kv.at[0, 0], load_sem.at[0]),
        pltpu.make_async_copy(v_hbm, kv.at[0, 1], load_sem.at[1]),
        pltpu.make_async_copy(w_hbm, w, load_sem.at[2]),
        pltpu.make_async_copy(q_hbm, q, load_sem.at[3]),
    ]
    for copy in loads:
        copy.start()

    barrier = pltpu.get_barrier_semaphore()
    near = [up, down] + [seq_at(z, y + k) for k in range(1, Y)]
    for partner in near:
        pl.semaphore_signal(barrier, inc=1, device_id={"seq": partner}, device_id_type=MESH)
    for k in range(1, H):
        pl.semaphore_signal(
            barrier, inc=1, device_id={"head": lax.rem(h + k, H)}, device_id_type=MESH
        )
    for g in range(128 // SEG):
        line = slot_ref[...] if g == 0 else pltpu.roll(slot_ref[...], 128 - SEG * g, 1)
        for i in range(T // 128):
            e = i * (128 // SEG) + g
            wanted[e] = line[i : i + 1, :] - e * T
    pl.semaphore_wait(barrier, len(near) + H - 1)
    loads[0].wait()
    loads[1].wait()

    def rows_of(i):
        return pl.ds(i * CR, CR)

    def zhop(i):
        return remote(
            kv.at[0, :, rows_of(i)], kv.at[Y, :, rows_of(i)],
            win_send.at[Y, i], win_recv.at[Y, i], up,
        )

    def spread(src, k, i):
        if k != 2:
            return [
                remote(
                    kv.at[src, :, rows_of(i)], kv.at[k, :, rows_of(i)],
                    win_send.at[k, i], win_recv.at[k, i], seq_at(z, y + k),
                )
            ]
        return [over(src, j, i) for j in range(2)]

    def over(src, j, i):
        return remote(
            kv.at[src, j, rows_of(i)], relay.at[j, rows_of(i)],
            relay_send.at[j, i], relay_recv.at[j, i], seq_at(z, y + (1 if j == 0 else -1)),
        )

    def forward(j, i):
        return remote(
            relay.at[j, rows_of(i)], kv.at[2, j, rows_of(i)],
            fwd_send.at[j, i], mid_recv.at[j, i], seq_at(z, y + (1 if j == 0 else -1)),
        )

    order = [1, 3, 2]
    zhop(0).start()
    for k in order:
        @pl.when(y + k < Y)
        def _():
            for i in range(CHUNKS):
                for copy in spread(0, k, i):
                    copy.start()

    def window_step(i):
        zhop(i).wait_recv()
        for k in order:
            @pl.when(y + k >= Y)
            def _():
                for copy in spread(Y, k, i):
                    copy.start()
        for j in range(2):
            over(0, j, i).wait_recv()
            forward(j, i).start()

    first_len = len_ref[0]
    lane_member = (s * T + lax.broadcasted_iota(jnp.int32, (1, T), 1)) < first_len
    loads[2].wait()
    keys = kv[0, 0]
    values = kv[0, 1]
    gate_pre = dot_t(w[0], keys)
    up_pre = dot_t(w[1], keys)
    sig_gate = jax.nn.sigmoid(gate_pre)
    gated = gate_pre * sig_gate
    activation = jnp.where(lane_member, gated * up_pre, 0.0).astype(bf16)
    back = jnp.where(lane_member, dot_t(w[2], values), 0.0)
    grad_up = (back * gated).astype(bf16)
    grad_gate = (back * up_pre * sig_gate * (1.0 + gate_pre * (1.0 - sig_gate))).astype(bf16)

    def chunk_of(zz):
        return lax.rem(zz + 2 * Z, Z)

    def piece(c, zz):
        return grad[c, pl.ds(pl.multiple_of(chunk_of(zz) * FR, FR), FR), :]

    def rs_up(t, c):
        return remote(
            rs_send_p.at[t, c], rs_recv_p.at[t, c], rsp_send.at[t, c], rsp_recv.at[t, c], up
        )

    def rs_down(t, c):
        return remote(
            rs_send_m.at[t, c], rs_recv_m.at[t, c], rsm_send.at[t, c], rsm_recv.at[t, c], down
        )

    def rs_step(t, c):
        if t < DOWN:
            value = piece(c, z - DOWN + t)
            if t > 0:
                rs_down(t - 1, c).wait_recv()
                value = value + rs_recv_m[t - 1, c].astype(f32)
            rs_send_m[t, c] = value.astype(bf16)
            rs_down(t, c).start()
        if t < UP:
            value = piece(c, z + UP - t)
            if t > 0:
                rs_up(t - 1, c).wait_recv()
                value = value + rs_recv_p[t - 1, c].astype(f32)
            rs_send_p[t, c] = value.astype(bf16)
            rs_up(t, c).start()

    grad[2] = dot_n(activation, values)
    rs_step(0, 2)
    grad[1] = dot_n(grad_up, keys)
    rs_step(0, 1)
    grad[0] = dot_n(grad_gate, keys)
    rs_step(0, 0)
    zhop(1).start()
    loads[3].wait()

    scale = 1.0 / math.sqrt(D)
    HALF = T // 2

    def attend(d, half):
        span = pl.ds(half * HALF, HALF)
        scores = dot_t(q[span, :], kv[d, 0]) * scale
        r = half * HALF + lax.broadcasted_iota(jnp.int32, (HALF, T), 0)
        col = lax.broadcasted_iota(jnp.int32, (HALF, T), 1)
        ahead = r - col + d * T
        allowed = (ahead >= 0) & (ahead < WIN) & (s * T - d * T + col >= 0)
        scores = jnp.where(allowed, scores, -jnp.inf)
        peak = jnp.max(scores, axis=1, keepdims=True)
        if d == 0:
            expo = jnp.exp(scores - peak)
            row_l[span, :] = jnp.broadcast_to(jnp.sum(expo, axis=1, keepdims=True), (HALF, 128))
            acc[span, :] = dot_n(expo.astype(bf16), kv[d, 1])
        else:
            before = row_m[span, :][:, 0:1]
            peak = jnp.maximum(before, peak)
            decay = jnp.exp(before - peak)
            expo = jnp.exp(scores - peak)
            row_l[span, :] = row_l[span, :] * decay + jnp.sum(expo, axis=1, keepdims=True)
            acc[span, :] = acc[span, :] * decay + dot_n(expo.astype(bf16), kv[d, 1])
        row_m[span, :] = jnp.broadcast_to(peak, (HALF, 128))

    def swiglu(inputs, gate_w, up_w, down_w):
        gate = dot_t(inputs, gate_w)
        hidden = (gate * jax.nn.sigmoid(gate) * dot_t(inputs, up_w)).astype(bf16)
        return dot_n(hidden, down_w).astype(bf16)

    def early_fast(half):
        span = pl.ds(half * HALF, HALF)
        first_out[span, :] = swiglu(q[span, :], w[0], w[1], w[2])

    fillers = [
        functools.partial(attend, 0, 0), functools.partial(attend, 0, 1),
        functools.partial(early_fast, 0), functools.partial(early_fast, 1),
    ]
    steps = max(UP, DOWN)
    hop, seen = 2, 0
    for t in range(1, steps):
        for c in (2, 1, 0):
            rs_step(t, c)
        if hop < CHUNKS:
            zhop(hop).start()
            hop += 1
        if seen < CHUNKS:
            window_step(seen)
            seen += 1
        if fillers:
            fillers.pop(0)()

    def y_copy(k, c):
        return remote(
            y_send.at[c], y_recv.at[k - 1, c], ys_send.at[k - 1, c], ys_recv.at[k - 1, c],
            seq_at(z, y + k),
        )

    for c in (2, 1, 0):
        value = piece(c, z)
        if DOWN > 0:
            rs_down(DOWN - 1, c).wait_recv()
            value = value + rs_recv_m[DOWN - 1, c].astype(f32)
        rs_up(UP - 1, c).wait_recv()
        value = value + rs_recv_p[UP - 1, c].astype(f32)
        total[c] = value
        y_send[c] = value.astype(bf16)
        for k in range(1, Y):
            y_copy(k, c).start()
    while hop < CHUNKS:
        zhop(hop).start()
        hop += 1
    while fillers:
        fillers.pop(0)()

    def idx_body(k, carry):
        target = lax.rem(s + k, N)
        remote(wanted.at[target], asked.at[s], idx_send, idx_recv, target).start()
        return carry

    group_count = jnp.full((1, D), first_len, jnp.int32).astype(f32)
    rate = lr_ref[0] / group_count
    for c in (2, 1, 0):
        value = total[c]
        for k in range(1, Y):
            y_copy(k, c).wait_recv()
            value = value + y_recv[k - 1, c].astype(f32)
        previous = w[c, pl.ds(pl.multiple_of(z * FR, FR), FR), :].astype(f32)
        updated = previous + rate * value
        old_norm = jnp.sqrt(jnp.sum(previous * previous, axis=1, keepdims=True) + eps)
        new_norm = jnp.sqrt(jnp.sum(updated * updated, axis=1, keepdims=True) + eps)
        new_w[z, c] = (updated * (old_norm / new_norm)).astype(bf16)

    def ag_up(t, c):
        at = chunk_of(z - t)
        return remote(new_w.at[at, c], new_w.at[at, c], agp_send.at[t, c], agp_recv.at[t, c], up)

    def ag_down(t, c):
        at = chunk_of(z + t)
        return remote(new_w.at[at, c], new_w.at[at, c], agm_send.at[t, c], agm_recv.at[t, c], down)

    def ag_wait_up(t, c):
        at = chunk_of(z - 1 - t)
        remote(
            new_w.at[at, c], new_w.at[at, c], agp_send.at[t, c], agp_recv.at[t, c], up
        ).wait_recv()

    def ag_wait_down(t, c):
        at = chunk_of(z + 1 + t)
        remote(
            new_w.at[at, c], new_w.at[at, c], agm_send.at[t, c], agm_recv.at[t, c], down
        ).wait_recv()

    def block_ready(d):
        for i in range(CHUNKS):
            if d == 2:
                for j in range(2):
                    forward(j, i).wait_recv()
            elif d != Y:
                spread(0, d, i)[0].wait_recv()

    def block(d, half):
        if half == 0:
            block_ready(d)
        attend(d, half)

    fillers = [functools.partial(block, d, half) for d in (Y, 1, 3, 2) for half in range(2)]
    for t in range(steps):
        for c in (2, 1, 0):
            if t < DOWN:
                if t > 0:
                    ag_wait_down(t - 1, c)
                ag_down(t, c).start()
            if t < UP:
                if t > 0:
                    ag_wait_up(t - 1, c)
                ag_up(t, c).start()
        if t == 0:
            lax.fori_loop(1, N, idx_body, 0)
            asked[s] = wanted[s]
        if seen < CHUNKS:
            window_step(seen)
            seen += 1
        elif fillers and t >= 2:
            fillers.pop(0)()
    while seen < CHUNKS:
        window_step(seen)
        seen += 1
    while fillers:
        fillers.pop(0)()
    pltpu.make_async_copy(asked.at[pl.ds(0, N - 1)], asked.at[pl.ds(0, N - 1)], idx_recv).wait()
    attention = (acc[...] / row_l[...][:, 0:1]).astype(bf16)
    for c in (2, 1, 0):
        if DOWN > 0:
            ag_wait_down(DOWN - 1, c)
        ag_wait_up(UP - 1, c)

    second = swiglu(
        q[...], new_w[:, 0].reshape(F, D), new_w[:, 1].reshape(F, D), new_w[:, 2].reshape(F, D)
    )
    member = (s * T + lax.broadcasted_iota(jnp.int32, (T, D), 0)) < first_len
    fast = jnp.where(member, first_out[...].astype(f32), second.astype(f32))
    summed = attention.astype(f32) + fast
    rows[...] = summed
    square = summed * summed
    coarse = square.astype(bf16)
    fine = (square - coarse.astype(f32)).astype(bf16)
    ones = jnp.ones((8, D), bf16)
    power[h] = (dot_t(ones, coarse) + dot_t(ones, fine))[0:1, :]

    def pow_copy(k):
        return pltpu.make_async_remote_copy(
            src_ref=power.at[h], dst_ref=power.at[h],
            send_sem=pow_send.at[k - 1], recv_sem=pow_recv.at[k - 1],
            device_id={"head": lax.rem(h + k, H)}, device_id_type=MESH,
        )

    for k in range(1, H):
        pow_copy(k).start()
    lines = jnp.broadcast_to(asked[...].astype(f32), (N, SEG, 128)).reshape(T, 128)
    lane = lax.broadcasted_iota(jnp.int32, (T, 128), 1)
    spot = lax.rem(lax.broadcasted_iota(jnp.int32, (T, 128), 0), SEG)
    picked = jnp.sum(jnp.where(lane == spot, lines, 0.0), axis=1, keepdims=True)
    column = lax.broadcasted_iota(jnp.int32, (T, T), 1).astype(f32)
    choose = jnp.where(column == picked, 1.0, 0.0).astype(bf16)
    for k in range(1, H):
        pow_copy(k).wait_recv()
    strength = power[0]
    for k in range(1, H):
        strength = strength + power[k]
    row_scale = lax.rsqrt(strength / (H * D) + eps)
    spread_scale = jnp.broadcast_to(row_scale, (128, T)).T
    wide_scale = jnp.concatenate([spread_scale] * (D // 128), axis=1)
    normed = (rows[...] * wide_scale * gain_ref[...]).astype(bf16)
    send_rows[...] = dot_n(choose, normed).reshape(N, SEG, D).astype(bf16)

    def a2a_body(k, carry):
        target = lax.rem(s + k, N)
        remote(send_rows.at[target], out_ref.at[s], a2a_send, a2a_recv, target).start()
        return carry

    lax.fori_loop(1, N, a2a_body, 0)
    own = pltpu.make_async_copy(send_rows.at[s], out_ref.at[s], own_sem)
    own.start()

    for i in range(CHUNKS):
        zhop(i).wait_send()
        for k in order:
            for copy in spread(0, k, i):
                copy.wait_send()
        for j in range(2):
            forward(j, i).wait_send()
    for c in range(3):
        for t in range(UP):
            rs_up(t, c).wait_send()
            ag_up(t, c).wait_send()
        for t in range(DOWN):
            rs_down(t, c).wait_send()
            ag_down(t, c).wait_send()
        for k in range(1, Y):
            y_copy(k, c).wait_send()
    for k in range(1, H):
        pow_copy(k).wait_send()
    pltpu.make_async_copy(wanted.at[pl.ds(0, N - 1)], wanted.at[pl.ds(0, N - 1)], idx_send).wait()
    own.wait()
    pltpu.make_async_copy(
        send_rows.at[pl.ds(0, N - 1)], send_rows.at[pl.ds(0, N - 1)], a2a_send
    ).wait()
    pltpu.make_async_copy(
        out_ref.at[pl.ds(0, N - 1)], out_ref.at[pl.ds(0, N - 1)], a2a_recv
    ).wait()


def solution(mesh, window=WINDOW):
    N = mesh.shape["seq"]
    H = mesh.shape["head"]

    def per_device(q, k, v, weights, learn_rate, out_gain, group_lengths, slot_order):
        T, _, D = q.shape
        F = weights.shape[0]
        Y = window // T
        Z = N // Y
        UP = Z // 2
        DOWN = Z - 1 - UP
        FR = F // Z
        SEG = T // N
        dma = pltpu.SemaphoreType.DMA
        VMEM = pltpu.VMEM
        any_spec = pl.BlockSpec(memory_space=pl.ANY)
        vmem_spec = pl.BlockSpec(memory_space=pltpu.VMEM)
        smem_spec = pl.BlockSpec(memory_space=pltpu.SMEM)
        out = pl.pallas_call(
            functools.partial(layer_kernel, Y, Z, H, UP, DOWN, window),
            out_shape=jax.ShapeDtypeStruct((N, SEG, D), bf16),
            in_specs=[any_spec] * 4 + [smem_spec, vmem_spec, smem_spec, vmem_spec],
            out_specs=any_spec,
            scratch_shapes=[
                VMEM((T, D), bf16),
                VMEM((Y + 1, 2, T, D), bf16),
                VMEM((3, F, D), bf16),
                VMEM((2, T, D), bf16),
                VMEM((3, F, D), f32),
                VMEM((UP, 3, FR, D), bf16),
                VMEM((max(DOWN, 1), 3, FR, D), bf16),
                VMEM((UP, 3, FR, D), bf16),
                VMEM((max(DOWN, 1), 3, FR, D), bf16),
                VMEM((3, FR, D), f32),
                VMEM((3, FR, D), bf16),
                VMEM((Y - 1, 3, FR, D), bf16),
                VMEM((Z, 3, FR, D), bf16),
                VMEM((T, D), f32),
                VMEM((T, 128), f32),
                VMEM((T, 128), f32),
                VMEM((T, D), bf16),
                VMEM((T, D), f32),
                VMEM((H, 1, T), f32),
                VMEM((N, 1, 128), jnp.int32),
                VMEM((N, 1, 128), jnp.int32),
                VMEM((N, SEG, D), bf16),
                dma((4,)),
                dma((Y + 1, CHUNKS)),
                dma((Y + 1, CHUNKS)),
                dma((2, CHUNKS)),
                dma((2, CHUNKS)),
                dma((2, CHUNKS)),
                dma((2, CHUNKS)),
                dma((UP, 3)),
                dma((UP, 3)),
                dma((max(DOWN, 1), 3)),
                dma((max(DOWN, 1), 3)),
                dma((Y - 1, 3)),
                dma((Y - 1, 3)),
                dma((UP, 3)),
                dma((UP, 3)),
                dma((max(DOWN, 1), 3)),
                dma((max(DOWN, 1), 3)),
                dma((max(H - 1, 1),)),
                dma((max(H - 1, 1),)),
                dma,
                dma,
                dma,
                dma,
                dma,
            ],
            compiler_params=pltpu.CompilerParams(
                collective_id=0, has_side_effects=True, vmem_limit_bytes=60 * 1024 * 1024
            ),
            name="ttt_layer",
        )(
            q.reshape(T, D), k.reshape(T, D), v.reshape(T, D),
            jnp.transpose(weights.reshape(F, 3, D), (1, 0, 2)),
            learn_rate, out_gain, group_lengths, slot_order.reshape(T // 128, 128),
        )
        return out.reshape(T, 1, D)

    return jax.shard_map(
        per_device,
        mesh=mesh,
        in_specs=(
            P("seq", "head", None),
            P("seq", "head", None),
            P("seq", "head", None),
            P(None, "head", None, None),
            P("head"),
            P("head", None),
            P(),
            P("seq"),
        ),
        out_specs=P("seq", "head", None),
        check_vma=False,
    )
```

time: 401 us -> 156 us (0.39)
  waiting for transfers between devices: 253 us -> 0 us
  Pallas kernels: 0 us -> 152 us
  blocking collectives: 60.8 us -> 0 us
  starting transfers between devices: 31.8 us -> 0 us
  matrix products: 14.6 us -> 0 us
  between operations: 14.4 us -> 0.66 us
  local copies, waits for them, and re-layouts: 15.4 us -> 1.87 us
  other arithmetic: 9.57 us -> 0 us
    psum x1 -> x0, waiting for transfers between devices: 162 us -> none  [fast_section(): summed = lax.psum(jnp.stack([term_gate, term_up, term_down], axis=2), 'seq')]
    pallas_call x0 -> x1, Pallas kernels: none -> 152 us  [per_device(): pl.pallas_call(functools.partial(layer_kernel, Y, Z, H, UP, DOWN, window)...]
    all_to_all x1 -> x0, waiting for transfers between devices: 91.3 us -> none  [per_device(): lax.all_to_all(wanted, 'seq', split_axis=0, concat_axis=0, tiled=True)]
    all_to_all x1 -> x0, blocking collectives: 40.2 us -> none  [per_device(): lax.all_to_all(gather_local(normed, asked_rows), 'seq', split_axis=0, con...]
    psum x1 -> x0, blocking collectives: 20.6 us -> none  [token_norm(): power = lax.psum(local_power, 'head')]
    ppermute x4 -> x0, starting transfers between devices: 17.3 us -> none  [shifted(): lax.ppermute(value, axis, [(source, source + steps) for source in range(f...]
    dot_general x11 -> x0, matrix products: 14.6 us -> none  [the longest x1 3.44 us: fast_section(): jnp.einsum('thd,fhcd->thcf', token_keys, fast_weights[:, :, 0:2, :], pref...]
    all_to_all x1 -> x0, starting transfers between devices: 14.4 us -> none  [per_device(): lax.all_to_all(wanted, 'seq', split_axis=0, concat_axis=0, tiled=True)]
  transfers between devices with their start and end apart: 6 -> 0, of which waited for: 2 -> 0; matrix products, arithmetic and copies ran while one was open for 5% -> 0% of each run, Pallas kernels for 0% -> 0%
where the time goes in v1:
time: 156 us; the launch traced here: 154 us
  Pallas kernels  152 us (97%)
  local copies, waits for them, and re-layouts  1.87 us (1%)
    pallas_call x1, Pallas kernels, per_device(): pl.pallas_call(functools.partial(layer_kernel, Y, Z, H, UP, DOWN, window)...  152 us

profile of v1, /device:TPU:1, one launch (start us, length us, event | category | flops | bytes accessed | tf_op | source)
XLA Modules:
  0.0 154.3 jit_solution(13712397365095040801)
XLA Ops:
  0.7 151.8 %ttt_layer.1 = bf16[64,8,512]{2,1,0:T(8,128)(2,1)} custom-call(bf16[512,512]{1,0:T(8,128)(2,1)} %bitcast.10, bf16[512,512]{1,0:T(8,128)(2,1)} %bitcast.11, bf16[512,512]{1,0:T(8,128)(2,1)} %bitcast.12, bf16[3,512,512]{2,1,0:T(8,128)(2,1)} %bitcast.9, f32[1]{0:T(128)S(6)} %copy.10.lr_ref, f32[1,512]{1,0:T(1,128)} %gain_ref.1, s32[2]{0:T(128)} %len_ref.1, ...), custom_call_target="tpu_custom_call" | custom-call | tf_op jit(solution)/shard_map/ttt_layer/pallas_call | solution.py:445
  152.5 1.9 %copy.11 = bf16[512,1,512]{2,0,1:T(8,128)(2,1)} copy(bf16[512,1,512]{2,0,1:T(8,128)(2,1)} %bitcast.8) | data formatting | bytes 1048576

commit v2 on v1

--- a/solution.py
+++ b/solution.py
@@ -9,7 +9,8 @@
 from jax.sharding import PartitionSpec as P
 
 WINDOW = 2048
-CHUNKS = 8
+CHUNKS = 16
+UP_HOPS = 6
 eps = 1e-06
 MESH = pl.DeviceIdType.MESH
 f32 = jnp.float32
@@ -30,7 +31,7 @@
     out_ref,
     q, kv, w, relay, grad, rs_send_p, rs_send_m, rs_recv_p, rs_recv_m,
     total, y_send, y_recv, new_w, acc, row_m, row_l, first_out, rows,
-    power, wanted, asked, send_rows,
+    power, wanted, asked, choose, send_rows,
     load_sem, win_send, win_recv, relay_send, relay_recv, fwd_send, mid_recv,
     rsp_send, rsp_recv, rsm_send, rsm_recv, ys_send, ys_recv,
     agp_send, agp_recv, agm_send, agm_recv,
@@ -94,17 +95,15 @@
             win_send.at[Y, i], win_recv.at[Y, i], up,
         )
 
-    def spread(src, k, i):
-        if k != 2:
-            return [
-                remote(
-                    kv.at[src, :, rows_of(i)], kv.at[k, :, rows_of(i)],
-                    win_send.at[k, i], win_recv.at[k, i], seq_at(z, y + k),
-                )
-            ]
-        return [over(src, j, i) for j in range(2)]
-
-    def over(src, j, i):
+    def spread(k, i):
+        src = jnp.where(y + k < Y, 0, Y)
+        return remote(
+            kv.at[src, :, rows_of(i)], kv.at[k, :, rows_of(i)],
+            win_send.at[k, i], win_recv.at[k, i], seq_at(z, y + k),
+        )
+
+    def over(j, i):
+        src = jnp.where(y + 2 < Y, 0, Y)
         return remote(
             kv.at[src, j, rows_of(i)], relay.at[j, rows_of(i)],
             relay_send.at[j, i], relay_recv.at[j, i], seq_at(z, y + (1 if j == 0 else -1)),
@@ -116,25 +115,23 @@
             fwd_send.at[j, i], mid_recv.at[j, i], seq_at(z, y + (1 if j == 0 else -1)),
         )
 
-    order = [1, 3, 2]
-    zhop(0).start()
-    for k in order:
-        @pl.when(y + k < Y)
-        def _():
-            for i in range(CHUNKS):
-                for copy in spread(0, k, i):
-                    copy.start()
+    AHEAD = 3
+    for i in range(AHEAD):
+        zhop(i).start()
 
     def window_step(i):
-        zhop(i).wait_recv()
-        for k in order:
-            @pl.when(y + k >= Y)
-            def _():
-                for copy in spread(Y, k, i):
-                    copy.start()
-        for j in range(2):
-            over(0, j, i).wait_recv()
-            forward(j, i).start()
+        if i < CHUNKS:
+            if i + AHEAD < CHUNKS:
+                zhop(i + AHEAD).start()
+            zhop(i).wait_recv()
+            for j in range(2):
+                over(j, i).start()
+            spread(1, i).start()
+            spread(3, i).start()
+        if 1 <= i <= CHUNKS:
+            for j in range(2):
+                over(j, i - 1).wait_recv()
+                forward(j, i - 1).start()
 
     first_len = len_ref[0]
     lane_member = (s * T + lax.broadcasted_iota(jnp.int32, (1, T), 1)) < first_len
@@ -184,36 +181,42 @@
 
     grad[2] = dot_n(activation, values)
     rs_step(0, 2)
+    window_step(0)
     grad[1] = dot_n(grad_up, keys)
     rs_step(0, 1)
+    window_step(1)
     grad[0] = dot_n(grad_gate, keys)
     rs_step(0, 0)
-    zhop(1).start()
     loads[3].wait()
 
-    scale = 1.0 / math.sqrt(D)
+    exponent = math.log2(math.e) / math.sqrt(D)
     HALF = T // 2
 
-    def attend(d, half):
-        span = pl.ds(half * HALF, HALF)
-        scores = dot_t(q[span, :], kv[d, 0]) * scale
-        r = half * HALF + lax.broadcasted_iota(jnp.int32, (HALF, T), 0)
-        col = lax.broadcasted_iota(jnp.int32, (HALF, T), 1)
-        ahead = r - col + d * T
-        allowed = (ahead >= 0) & (ahead < WIN) & (s * T - d * T + col >= 0)
-        scores = jnp.where(allowed, scores, -jnp.inf)
+    def attend(d, kh, qh):
+        span = pl.ds(qh * HALF, HALF)
+        part = pl.ds(kh * HALF, HALF)
+        scores = dot_t(q[span, :], kv[d, 0, part, :])
+        if d in (0, Y):
+            behind = (
+                lax.broadcasted_iota(jnp.int32, (HALF, HALF), 0)
+                - lax.broadcasted_iota(jnp.int32, (HALF, HALF), 1)
+                + ((qh - kh) * HALF + d * T)
+            )
+            scores = jnp.where((behind >= 0) & (behind < WIN), scores, -jnp.inf)
+        if d > 0:
+            scores = scores + jnp.where(s >= d, 0.0, -jnp.inf)
         peak = jnp.max(scores, axis=1, keepdims=True)
-        if d == 0:
-            expo = jnp.exp(scores - peak)
+        if d == 0 and kh == 0:
+            expo = jnp.exp2((scores - peak) * exponent)
             row_l[span, :] = jnp.broadcast_to(jnp.sum(expo, axis=1, keepdims=True), (HALF, 128))
-            acc[span, :] = dot_n(expo.astype(bf16), kv[d, 1])
+            acc[span, :] = dot_n(expo.astype(bf16), kv[d, 1, part, :])
         else:
             before = row_m[span, :][:, 0:1]
             peak = jnp.maximum(before, peak)
-            decay = jnp.exp(before - peak)
-            expo = jnp.exp(scores - peak)
+            decay = jnp.exp2((before - peak) * exponent)
+            expo = jnp.exp2((scores - peak) * exponent)
             row_l[span, :] = row_l[span, :] * decay + jnp.sum(expo, axis=1, keepdims=True)
-            acc[span, :] = acc[span, :] * decay + dot_n(expo.astype(bf16), kv[d, 1])
+            acc[span, :] = acc[span, :] * decay + dot_n(expo.astype(bf16), kv[d, 1, part, :])
         row_m[span, :] = jnp.broadcast_to(peak, (HALF, 128))
 
     def swiglu(inputs, gate_w, up_w, down_w):
@@ -221,25 +224,20 @@
         hidden = (gate * jax.nn.sigmoid(gate) * dot_t(inputs, up_w)).astype(bf16)
         return dot_n(hidden, down_w).astype(bf16)
 
-    def early_fast(half):
-        span = pl.ds(half * HALF, HALF)
+    def early_fast(part):
+        span = pl.ds(part * (T // 4), T // 4)
         first_out[span, :] = swiglu(q[span, :], w[0], w[1], w[2])
 
-    fillers = [
-        functools.partial(attend, 0, 0), functools.partial(attend, 0, 1),
-        functools.partial(early_fast, 0), functools.partial(early_fast, 1),
-    ]
+    fillers = [functools.partial(attend, 0, 0, qh) for qh in range(2)]
+    fillers += [functools.partial(attend, 0, 1, qh) for qh in range(1, 2)]
+    fillers += [functools.partial(early_fast, part) for part in range(4)]
     steps = max(UP, DOWN)
-    hop, seen = 2, 0
+    seen = 2
     for t in range(1, steps):
         for c in (2, 1, 0):
             rs_step(t, c)
-        if hop < CHUNKS:
-            zhop(hop).start()
-            hop += 1
-        if seen < CHUNKS:
-            window_step(seen)
-            seen += 1
+        window_step(seen)
+        seen += 1
         if fillers:
             fillers.pop(0)()
 
@@ -260,9 +258,6 @@
         y_send[c] = value.astype(bf16)
         for k in range(1, Y):
             y_copy(k, c).start()
-    while hop < CHUNKS:
-        zhop(hop).start()
-        hop += 1
     while fillers:
         fillers.pop(0)()
 
@@ -304,20 +299,24 @@
             new_w.at[at, c], new_w.at[at, c], agm_send.at[t, c], agm_recv.at[t, c], down
         ).wait_recv()
 
-    def block_ready(d):
-        for i in range(CHUNKS):
+    def block_ready(d, kh):
+        for i in range(kh * CHUNKS // 2, (kh + 1) * CHUNKS // 2):
             if d == 2:
                 for j in range(2):
                     forward(j, i).wait_recv()
             elif d != Y:
-                spread(0, d, i)[0].wait_recv()
-
-    def block(d, half):
-        if half == 0:
-            block_ready(d)
-        attend(d, half)
-
-    fillers = [functools.partial(block, d, half) for d in (Y, 1, 3, 2) for half in range(2)]
+                spread(d, i).wait_recv()
+
+    def block(d, kh, qh):
+        if qh == 0:
+            block_ready(d, kh)
+        attend(d, kh, qh)
+
+    fillers = [
+        functools.partial(block, d, kh, qh)
+        for kh in range(2) for d in (Y, 1, 3, 2) for qh in range(2)
+        if (d, kh, qh) != (Y, 0, 1)
+    ]
     for t in range(steps):
         for c in (2, 1, 0):
             if t < DOWN:
@@ -331,18 +330,26 @@
         if t == 0:
             lax.fori_loop(1, N, idx_body, 0)
             asked[s] = wanted[s]
-        if seen < CHUNKS:
+        if seen <= CHUNKS:
             window_step(seen)
             seen += 1
-        elif fillers and t >= 2:
-            fillers.pop(0)()
-    while seen < CHUNKS:
+        for _ in range(1 if t < 6 else 2):
+            if fillers and seen > (CHUNKS if len(fillers) <= 8 else CHUNKS // 2):
+                fillers.pop(0)()
+    while seen <= CHUNKS:
         window_step(seen)
         seen += 1
     while fillers:
         fillers.pop(0)()
     pltpu.make_async_copy(asked.at[pl.ds(0, N - 1)], asked.at[pl.ds(0, N - 1)], idx_recv).wait()
     attention = (acc[...] / row_l[...][:, 0:1]).astype(bf16)
+    lines = jnp.broadcast_to(asked[...].astype(f32), (N, SEG, 128)).reshape(T, 128)
+    lane = lax.broadcasted_iota(jnp.int32, (T, 128), 1)
+    spot = lax.rem(lax.broadcasted_iota(jnp.int32, (T, 128), 0), SEG)
+    picked = jnp.sum(jnp.where(lane == spot, lines, 0.0), axis=1, keepdims=True)
+    column = lax.broadcasted_iota(jnp.int32, (T, T), 1).astype(f32)
+    choose[...] = jnp.where(column == picked, 1.0, 0.0).astype(bf16)
+    rows[...] = dot_n(choose[...], attention)
     for c in (2, 1, 0):
         if DOWN > 0:
             ag_wait_down(DOWN - 1, c)
@@ -354,7 +361,6 @@
     member = (s * T + lax.broadcasted_iota(jnp.int32, (T, D), 0)) < first_len
     fast = jnp.where(member, first_out[...].astype(f32), second.astype(f32))
     summed = attention.astype(f32) + fast
-    rows[...] = summed
     square = summed * summed
     coarse = square.astype(bf16)
     fine = (square - coarse.astype(f32)).astype(bf16)
@@ -370,38 +376,43 @@
 
     for k in range(1, H):
         pow_copy(k).start()
-    lines = jnp.broadcast_to(asked[...].astype(f32), (N, SEG, 128)).reshape(T, 128)
-    lane = lax.broadcasted_iota(jnp.int32, (T, 128), 1)
-    spot = lax.rem(lax.broadcasted_iota(jnp.int32, (T, 128), 0), SEG)
-    picked = jnp.sum(jnp.where(lane == spot, lines, 0.0), axis=1, keepdims=True)
-    column = lax.broadcasted_iota(jnp.int32, (T, T), 1).astype(f32)
-    choose = jnp.where(column == picked, 1.0, 0.0).astype(bf16)
+    rows[...] = rows[...] + dot_n(choose[...], fast.astype(bf16))
     for k in range(1, H):
         pow_copy(k).wait_recv()
     strength = power[0]
     for k in range(1, H):
         strength = strength + power[k]
     row_scale = lax.rsqrt(strength / (H * D) + eps)
-    spread_scale = jnp.broadcast_to(row_scale, (128, T)).T
-    wide_scale = jnp.concatenate([spread_scale] * (D // 128), axis=1)
-    normed = (rows[...] * wide_scale * gain_ref[...]).astype(bf16)
-    send_rows[...] = dot_n(choose, normed).reshape(N, SEG, D).astype(bf16)
-
-    def a2a_body(k, carry):
-        target = lax.rem(s + k, N)
-        remote(send_rows.at[target], out_ref.at[s], a2a_send, a2a_recv, target).start()
-        return carry
-
-    lax.fori_loop(1, N, a2a_body, 0)
+
+    GROUPS = 4
+    NG = N // GROUPS
+    TG = T // GROUPS
+    for far in (2, 1, 3, 0):
+        g = lax.rem(s // NG + far, GROUPS)
+        span = pl.ds(pl.multiple_of(g * TG, TG), TG)
+        factor = jnp.sum(choose[span, :].astype(f32) * row_scale, axis=1, keepdims=True)
+        normed = rows[span, :] * factor * gain_ref[...]
+        send_rows[pl.ds(g * NG, NG)] = normed.reshape(NG, SEG, D).astype(bf16)
+
+        def a2a_body(k, carry):
+            target = g * NG + k
+
+            @pl.when(target != s)
+            def _():
+                remote(send_rows.at[target], out_ref.at[s], a2a_send, a2a_recv, target).start()
+
+            return carry
+
+        lax.fori_loop(0, NG, a2a_body, 0)
     own = pltpu.make_async_copy(send_rows.at[s], out_ref.at[s], own_sem)
     own.start()
 
     for i in range(CHUNKS):
         zhop(i).wait_send()
-        for k in order:
-            for copy in spread(0, k, i):
-                copy.wait_send()
+        spread(1, i).wait_send()
+        spread(3, i).wait_send()
         for j in range(2):
+            over(j, i).wait_send()
             forward(j, i).wait_send()
     for c in range(3):
         for t in range(UP):
@@ -433,7 +444,7 @@
         F = weights.shape[0]
         Y = window // T
         Z = N // Y
-        UP = Z // 2
+        UP = min(UP_HOPS, Z // 2)
         DOWN = Z - 1 - UP
         FR = F // Z
         SEG = T // N
@@ -469,6 +480,7 @@
                 VMEM((H, 1, T), f32),
                 VMEM((N, 1, 128), jnp.int32),
                 VMEM((N, 1, 128), jnp.int32),
+                VMEM((T, T), bf16),
                 VMEM((N, SEG, D), bf16),
                 dma((4,)),
                 dma((Y + 1, CHUNKS)),

time: 156 us -> 127 us (0.81)
  Pallas kernels: 152 us -> 124 us
    pallas_call x1, Pallas kernels: 152 us -> 124 us  [per_device(): pl.pallas_call(functools.partial(layer_kernel, Y, Z, H, UP, DOWN, window)...]
where the time goes in v2:
time: 127 us
  Pallas kernels  124 us (98%)
  local copies, waits for them, and re-layouts  1.87 us (1%)
    pallas_call x1, Pallas kernels, per_device(): pl.pallas_call(functools.partial(layer_kernel, Y, Z, H, UP, DOWN, window)...  124 us

profile of v2, /device:TPU:1, one launch (start us, length us, event | category | flops | bytes accessed | tf_op | source)
XLA Modules:
  0.0 126.6 jit_solution(5109276649559382685)
XLA Ops:
  0.7 124.1 %ttt_layer.1 = bf16[64,8,512]{2,1,0:T(8,128)(2,1)} custom-call(bf16[512,512]{1,0:T(8,128)(2,1)} %bitcast.10, bf16[512,512]{1,0:T(8,128)(2,1)} %bitcast.11, bf16[512,512]{1,0:T(8,128)(2,1)} %bitcast.12, bf16[3,512,512]{2,1,0:T(8,128)(2,1)} %bitcast.9, f32[1]{0:T(128)S(6)} %copy.10.lr_ref, f32[1,512]{1,0:T(1,128)} %gain_ref.1, s32[2]{0:T(128)} %len_ref.1, ...), custom_call_target="tpu_custom_call" | custom-call | tf_op jit(solution)/shard_map/ttt_layer/pallas_call | solution.py:456
  124.8 1.9 %copy.11 = bf16[512,1,512]{2,0,1:T(8,128)(2,1)} copy(bf16[512,1,512]{2,0,1:T(8,128)(2,1)} %bitcast.8) | data formatting | bytes 1048576

commit v3 on v2

--- a/solution.py
+++ b/solution.py
@@ -10,7 +10,8 @@
 
 WINDOW = 2048
 CHUNKS = 16
-UP_HOPS = 6
+UP_HOPS = 7
+SUB = 1
 eps = 1e-06
 MESH = pl.DeviceIdType.MESH
 f32 = jnp.float32
@@ -150,43 +151,58 @@
     def chunk_of(zz):
         return lax.rem(zz + 2 * Z, Z)
 
-    def piece(c, zz):
-        return grad[c, pl.ds(pl.multiple_of(chunk_of(zz) * FR, FR), FR), :]
-
-    def rs_up(t, c):
-        return remote(
-            rs_send_p.at[t, c], rs_recv_p.at[t, c], rsp_send.at[t, c], rsp_recv.at[t, c], up
-        )
-
-    def rs_down(t, c):
-        return remote(
-            rs_send_m.at[t, c], rs_recv_m.at[t, c], rsm_send.at[t, c], rsm_recv.at[t, c], down
-        )
-
-    def rs_step(t, c):
+    HR = FR // SUB
+    units = [(c, b) for c in (2, 1, 0) for b in range(SUB)]
+
+    def at_rows(u):
+        return pl.ds(u[1] * HR, HR)
+
+    def slot(u):
+        return u[0] * SUB + u[1]
+
+    def piece(u, zz):
+        first = pl.multiple_of(chunk_of(zz) * FR + u[1] * HR, HR)
+        return grad[u[0], pl.ds(first, HR), :]
+
+    def rs_up(t, u):
+        return remote(
+            rs_send_p.at[t, u[0], at_rows(u)], rs_recv_p.at[t, u[0], at_rows(u)],
+            rsp_send.at[t, slot(u)], rsp_recv.at[t, slot(u)], up,
+        )
+
+    def rs_down(t, u):
+        return remote(
+            rs_send_m.at[t, u[0], at_rows(u)], rs_recv_m.at[t, u[0], at_rows(u)],
+            rsm_send.at[t, slot(u)], rsm_recv.at[t, slot(u)], down,
+        )
+
+    def rs_step(t, u):
         if t < DOWN:
-            value = piece(c, z - DOWN + t)
+            value = piece(u, z - DOWN + t)
             if t > 0:
-                rs_down(t - 1, c).wait_recv()
-                value = value + rs_recv_m[t - 1, c].astype(f32)
-            rs_send_m[t, c] = value.astype(bf16)
-            rs_down(t, c).start()
+                rs_down(t - 1, u).wait_recv()
+                value = value + rs_recv_m[t - 1, u[0], at_rows(u)].astype(f32)
+            rs_send_m[t, u[0], at_rows(u)] = value.astype(bf16)
+            rs_down(t, u).start()
         if t < UP:
-            value = piece(c, z + UP - t)
+            value = piece(u, z + UP - t)
             if t > 0:
-                rs_up(t - 1, c).wait_recv()
-                value = value + rs_recv_p[t - 1, c].astype(f32)
-            rs_send_p[t, c] = value.astype(bf16)
-            rs_up(t, c).start()
+                rs_up(t - 1, u).wait_recv()
+                value = value + rs_recv_p[t - 1, u[0], at_rows(u)].astype(f32)
+            rs_send_p[t, u[0], at_rows(u)] = value.astype(bf16)
+            rs_up(t, u).start()
 
     grad[2] = dot_n(activation, values)
-    rs_step(0, 2)
+    for b in range(SUB):
+        rs_step(0, (2, b))
     window_step(0)
     grad[1] = dot_n(grad_up, keys)
-    rs_step(0, 1)
+    for b in range(SUB):
+        rs_step(0, (1, b))
     window_step(1)
     grad[0] = dot_n(grad_gate, keys)
-    rs_step(0, 0)
+    for b in range(SUB):
+        rs_step(0, (0, b))
     loads[3].wait()
 
     exponent = math.log2(math.e) / math.sqrt(D)
@@ -229,13 +245,13 @@
         first_out[span, :] = swiglu(q[span, :], w[0], w[1], w[2])
 
     fillers = [functools.partial(attend, 0, 0, qh) for qh in range(2)]
-    fillers += [functools.partial(attend, 0, 1, qh) for qh in range(1, 2)]
+    fillers += [functools.partial(attend, 0, 1, 1)]
     fillers += [functools.partial(early_fast, part) for part in range(4)]
     steps = max(UP, DOWN)
     seen = 2
     for t in range(1, steps):
-        for c in (2, 1, 0):
-            rs_step(t, c)
+        for u in units:
+            rs_step(t, u)
         window_step(seen)
         seen += 1
         if fillers:
@@ -248,13 +264,14 @@
         )
 
     for c in (2, 1, 0):
-        value = piece(c, z)
-        if DOWN > 0:
-            rs_down(DOWN - 1, c).wait_recv()
-            value = value + rs_recv_m[DOWN - 1, c].astype(f32)
-        rs_up(UP - 1, c).wait_recv()
-        value = value + rs_recv_p[UP - 1, c].astype(f32)
-        total[c] = value
+        for b in range(SUB):
+            u = (c, b)
+            value = piece(u, z)
+            rs_down(DOWN - 1, u).wait_recv()
+            value = value + rs_recv_m[DOWN - 1, c, at_rows(u)].astype(f32)
+            rs_up(UP - 1, u).wait_recv()
+            total[c, at_rows(u)] = value + rs_recv_p[UP - 1, c, at_rows(u)].astype(f32)
+        value = total[c]
         y_send[c] = value.astype(bf16)
         for k in range(1, Y):
             y_copy(k, c).start()
@@ -279,25 +296,21 @@
         new_norm = jnp.sqrt(jnp.sum(updated * updated, axis=1, keepdims=True) + eps)
         new_w[z, c] = (updated * (old_norm / new_norm)).astype(bf16)
 
-    def ag_up(t, c):
-        at = chunk_of(z - t)
-        return remote(new_w.at[at, c], new_w.at[at, c], agp_send.at[t, c], agp_recv.at[t, c], up)
-
-    def ag_down(t, c):
-        at = chunk_of(z + t)
-        return remote(new_w.at[at, c], new_w.at[at, c], agm_send.at[t, c], agm_recv.at[t, c], down)
-
-    def ag_wait_up(t, c):
-        at = chunk_of(z - 1 - t)
-        remote(
-            new_w.at[at, c], new_w.at[at, c], agp_send.at[t, c], agp_recv.at[t, c], up
-        ).wait_recv()
-
-    def ag_wait_down(t, c):
-        at = chunk_of(z + 1 + t)
-        remote(
-            new_w.at[at, c], new_w.at[at, c], agm_send.at[t, c], agm_recv.at[t, c], down
-        ).wait_recv()
+    def ag_copy(at, t, u, ssem, rsem, seq):
+        part = new_w.at[at, u[0], at_rows(u)]
+        return remote(part, part, ssem.at[t, slot(u)], rsem.at[t, slot(u)], seq)
+
+    def ag_up(t, u):
+        return ag_copy(chunk_of(z - t), t, u, agp_send, agp_recv, up)
+
+    def ag_down(t, u):
+        return ag_copy(chunk_of(z + t), t, u, agm_send, agm_recv, down)
+
+    def ag_wait_up(t, u):
+        ag_copy(chunk_of(z - 1 - t), t, u, agp_send, agp_recv, up).wait_recv()
+
+    def ag_wait_down(t, u):
+        ag_copy(chunk_of(z + 1 + t), t, u, agm_send, agm_recv, down).wait_recv()
 
     def block_ready(d, kh):
         for i in range(kh * CHUNKS // 2, (kh + 1) * CHUNKS // 2):
@@ -317,47 +330,75 @@
         for kh in range(2) for d in (Y, 1, 3, 2) for qh in range(2)
         if (d, kh, qh) != (Y, 0, 1)
     ]
+    def find_rows():
+        pltpu.make_async_copy(
+            asked.at[pl.ds(0, N - 1)], asked.at[pl.ds(0, N - 1)], idx_recv
+        ).wait()
+        lines = jnp.broadcast_to(asked[...].astype(f32), (N, SEG, 128)).reshape(T, 128)
+        lane = lax.broadcasted_iota(jnp.int32, (T, 128), 1)
+        spot = lax.rem(lax.broadcasted_iota(jnp.int32, (T, 128), 0), SEG)
+        picked = jnp.sum(jnp.where(lane == spot, lines, 0.0), axis=1, keepdims=True)
+        column = lax.broadcasted_iota(jnp.int32, (T, T), 1).astype(f32)
+        choose[...] = jnp.where(column == picked, 1.0, 0.0).astype(bf16)
+
+    near_set = list(range(-((Z // 2) // 2), (Z // 2) - (Z // 2) // 2))
+    far_set = [o for o in range(-UP, DOWN + 1) if o not in near_set]
+
+    def partial_fast(offsets):
+        gate_w, up_w, down_w = (
+            jnp.concatenate([new_w[chunk_of(z + o), c] for o in offsets], axis=0) for c in range(3)
+        )
+        gate = dot_t(q[...], gate_w)
+        hidden = (gate * jax.nn.sigmoid(gate) * dot_t(q[...], up_w)).astype(bf16)
+        return dot_n(hidden, down_w)
+
+    def near_fast():
+        rows[...] = partial_fast(near_set)
+
+    extra = [find_rows]
     for t in range(steps):
-        for c in (2, 1, 0):
+        for u in units:
             if t < DOWN:
                 if t > 0:
-                    ag_wait_down(t - 1, c)
-                ag_down(t, c).start()
+                    ag_wait_down(t - 1, u)
+                ag_down(t, u).start()
             if t < UP:
                 if t > 0:
-                    ag_wait_up(t - 1, c)
-                ag_up(t, c).start()
+                    ag_wait_up(t - 1, u)
+                ag_up(t, u).start()
         if t == 0:
             lax.fori_loop(1, N, idx_body, 0)
             asked[s] = wanted[s]
-        if seen <= CHUNKS:
-            window_step(seen)
-            seen += 1
-        for _ in range(1 if t < 6 else 2):
+        for _ in range(1):
+            if seen <= CHUNKS:
+                window_step(seen)
+                seen += 1
+        for _ in range(2):
             if fillers and seen > (CHUNKS if len(fillers) <= 8 else CHUNKS // 2):
                 fillers.pop(0)()
+        if t == steps - 3:
+            find_rows()
+            extra.clear()
     while seen <= CHUNKS:
         window_step(seen)
         seen += 1
     while fillers:
         fillers.pop(0)()
-    pltpu.make_async_copy(asked.at[pl.ds(0, N - 1)], asked.at[pl.ds(0, N - 1)], idx_recv).wait()
+    for step in extra:
+        step()
+    if steps <= 2:
+        for u in units:
+            ag_wait_down(DOWN - 1, u)
+            ag_wait_up(UP - 1, u)
+    near_fast()
     attention = (acc[...] / row_l[...][:, 0:1]).astype(bf16)
-    lines = jnp.broadcast_to(asked[...].astype(f32), (N, SEG, 128)).reshape(T, 128)
-    lane = lax.broadcasted_iota(jnp.int32, (T, 128), 1)
-    spot = lax.rem(lax.broadcasted_iota(jnp.int32, (T, 128), 0), SEG)
-    picked = jnp.sum(jnp.where(lane == spot, lines, 0.0), axis=1, keepdims=True)
-    column = lax.broadcasted_iota(jnp.int32, (T, T), 1).astype(f32)
-    choose[...] = jnp.where(column == picked, 1.0, 0.0).astype(bf16)
-    rows[...] = dot_n(choose[...], attention)
-    for c in (2, 1, 0):
-        if DOWN > 0:
-            ag_wait_down(DOWN - 1, c)
-        ag_wait_up(UP - 1, c)
-
-    second = swiglu(
-        q[...], new_w[:, 0].reshape(F, D), new_w[:, 1].reshape(F, D), new_w[:, 2].reshape(F, D)
-    )
+    acc[...] = dot_n(choose[...], attention)
+    if steps > 2:
+        for u in units:
+            ag_wait_down(DOWN - 1, u)
+            ag_wait_up(UP - 1, u)
+
+    second = (rows[...] + partial_fast(far_set)).astype(bf16)
     member = (s * T + lax.broadcasted_iota(jnp.int32, (T, D), 0)) < first_len
     fast = jnp.where(member, first_out[...].astype(f32), second.astype(f32))
     summed = attention.astype(f32) + fast
@@ -376,7 +417,7 @@
 
     for k in range(1, H):
         pow_copy(k).start()
-    rows[...] = rows[...] + dot_n(choose[...], fast.astype(bf16))
+    rows[...] = acc[...] + dot_n(choose[...], fast.astype(bf16))
     for k in range(1, H):
         pow_copy(k).wait_recv()
     strength = power[0]
@@ -414,13 +455,14 @@
         for j in range(2):
             over(j, i).wait_send()
             forward(j, i).wait_send()
+    for u in units:
+        for t in range(UP):
+            rs_up(t, u).wait_send()
+            ag_up(t, u).wait_send()
+        for t in range(DOWN):
+            rs_down(t, u).wait_send()
+            ag_down(t, u).wait_send()
     for c in range(3):
-        for t in range(UP):
-            rs_up(t, c).wait_send()
-            ag_up(t, c).wait_send()
-        for t in range(DOWN):
-            rs_down(t, c).wait_send()
-            ag_down(t, c).wait_send()
         for k in range(1, Y):
             y_copy(k, c).wait_send()
     for k in range(1, H):
@@ -489,16 +531,16 @@
                 dma((2, CHUNKS)),
                 dma((2, CHUNKS)),
                 dma((2, CHUNKS)),
-                dma((UP, 3)),
-                dma((UP, 3)),
-                dma((max(DOWN, 1), 3)),
-                dma((max(DOWN, 1), 3)),
+                dma((UP, 3 * SUB)),
+                dma((UP, 3 * SUB)),
+                dma((max(DOWN, 1), 3 * SUB)),
+                dma((max(DOWN, 1), 3 * SUB)),
                 dma((Y - 1, 3)),
                 dma((Y - 1, 3)),
-                dma((UP, 3)),
-                dma((UP, 3)),
-                dma((max(DOWN, 1), 3)),
-                dma((max(DOWN, 1), 3)),
+                dma((UP, 3 * SUB)),
+                dma((UP, 3 * SUB)),
+                dma((max(DOWN, 1), 3 * SUB)),
+                dma((max(DOWN, 1), 3 * SUB)),
                 dma((max(H - 1, 1),)),
                 dma((max(H - 1, 1),)),
                 dma,

time: 127 us -> 122 us (0.961)
  Pallas kernels: 124 us -> 120 us
    pallas_call x1, Pallas kernels: 124 us -> 120 us  [per_device(): pl.pallas_call(functools.partial(layer_kernel, Y, Z, H, UP, DOWN, window)...]
where the time goes in v3:
time: 122 us
  Pallas kernels  120 us (98%)
  local copies, waits for them, and re-layouts  1.87 us (2%)
    pallas_call x1, Pallas kernels, per_device(): pl.pallas_call(functools.partial(layer_kernel, Y, Z, H, UP, DOWN, window)...  120 us

profile of v3, /device:TPU:1, one launch (start us, length us, event | category | flops | bytes accessed | tf_op | source)
XLA Modules:
  0.0 122.3 jit_solution(5309607645062191488)
XLA Ops:
  0.7 119.8 %ttt_layer.1 = bf16[64,8,512]{2,1,0:T(8,128)(2,1)} custom-call(bf16[512,512]{1,0:T(8,128)(2,1)} %bitcast.10, bf16[512,512]{1,0:T(8,128)(2,1)} %bitcast.11, bf16[512,512]{1,0:T(8,128)(2,1)} %bitcast.12, bf16[3,512,512]{2,1,0:T(8,128)(2,1)} %bitcast.9, f32[1]{0:T(128)S(6)} %copy.10.lr_ref, f32[1,512]{1,0:T(1,128)} %gain_ref.1, s32[2]{0:T(128)} %len_ref.1, ...), custom_call_target="tpu_custom_call" | custom-call | tf_op jit(solution)/shard_map/ttt_layer/pallas_call | solution.py:498
  120.4 1.9 %copy.11 = bf16[512,1,512]{2,0,1:T(8,128)(2,1)} copy(bf16[512,1,512]{2,0,1:T(8,128)(2,1)} %bitcast.8) | data formatting | bytes 1048576

commit v4 on v3

--- a/solution.py
+++ b/solution.py
@@ -32,7 +32,7 @@
     out_ref,
     q, kv, w, relay, grad, rs_send_p, rs_send_m, rs_recv_p, rs_recv_m,
     total, y_send, y_recv, new_w, acc, row_m, row_l, first_out, rows,
-    power, wanted, asked, choose, send_rows,
+    power, wanted, asked, choose, terms, send_rows,
     load_sem, win_send, win_recv, relay_send, relay_recv, fwd_send, mid_recv,
     rsp_send, rsp_recv, rsm_send, rsm_recv, ys_send, ys_recv,
     agp_send, agp_recv, agm_send, agm_recv,
@@ -137,17 +137,6 @@
     first_len = len_ref[0]
     lane_member = (s * T + lax.broadcasted_iota(jnp.int32, (1, T), 1)) < first_len
     loads[2].wait()
-    keys = kv[0, 0]
-    values = kv[0, 1]
-    gate_pre = dot_t(w[0], keys)
-    up_pre = dot_t(w[1], keys)
-    sig_gate = jax.nn.sigmoid(gate_pre)
-    gated = gate_pre * sig_gate
-    activation = jnp.where(lane_member, gated * up_pre, 0.0).astype(bf16)
-    back = jnp.where(lane_member, dot_t(w[2], values), 0.0)
-    grad_up = (back * gated).astype(bf16)
-    grad_gate = (back * up_pre * sig_gate * (1.0 + gate_pre * (1.0 - sig_gate))).astype(bf16)
-
     def chunk_of(zz):
         return lax.rem(zz + 2 * Z, Z)
 
@@ -192,17 +181,39 @@
             rs_send_p[t, u[0], at_rows(u)] = value.astype(bf16)
             rs_up(t, u).start()
 
-    grad[2] = dot_n(activation, values)
-    for b in range(SUB):
-        rs_step(0, (2, b))
+    early = list(range(Z // 4, Z // 4 + Z // 2))
+    late = list(range(-(Z // 4), Z // 2 - Z // 4))
+
+    def hidden_terms(offsets):
+        gate_w, up_w, down_w = (
+            jnp.concatenate(
+                [w[c, pl.ds(pl.multiple_of(chunk_of(z + o) * FR, FR), FR), :] for o in offsets],
+                axis=0,
+            )
+            for c in range(3)
+        )
+        gate_pre = dot_t(gate_w, kv[0, 0])
+        up_pre = dot_t(up_w, kv[0, 0])
+        sig_gate = jax.nn.sigmoid(gate_pre)
+        gated = gate_pre * sig_gate
+        terms[2] = jnp.where(lane_member, gated * up_pre, 0.0).astype(bf16)
+        back = jnp.where(lane_member, dot_t(down_w, kv[0, 1]), 0.0)
+        terms[1] = (back * gated).astype(bf16)
+        terms[0] = (back * up_pre * sig_gate * (1.0 + gate_pre * (1.0 - sig_gate))).astype(bf16)
+
+    def weight_terms(offsets, c):
+        value = dot_n(terms[c], kv[0, 1 if c == 2 else 0])
+        for i, o in enumerate(offsets):
+            first = pl.multiple_of(chunk_of(z + o) * FR, FR)
+            grad[c, pl.ds(first, FR), :] = value[i * FR : (i + 1) * FR, :]
+
+    hidden_terms(early)
+    for c in (2, 1, 0):
+        weight_terms(early, c)
+        for b in range(SUB):
+            rs_step(0, (c, b))
     window_step(0)
-    grad[1] = dot_n(grad_up, keys)
-    for b in range(SUB):
-        rs_step(0, (1, b))
     window_step(1)
-    grad[0] = dot_n(grad_gate, keys)
-    for b in range(SUB):
-        rs_step(0, (0, b))
     loads[3].wait()
 
     exponent = math.log2(math.e) / math.sqrt(D)
@@ -254,8 +265,16 @@
             rs_step(t, u)
         window_step(seen)
         seen += 1
-        if fillers:
+        if t == 1:
+            hidden_terms(late)
+        elif t == 2:
+            for c in (2, 1, 0):
+                weight_terms(late, c)
+        elif fillers:
             fillers.pop(0)()
+    if steps < 3:
+        for c in (2, 1, 0):
+            weight_terms(late, c)
 
     def y_copy(k, c):
         return remote(
@@ -523,6 +542,7 @@
                 VMEM((N, 1, 128), jnp.int32),
                 VMEM((N, 1, 128), jnp.int32),
                 VMEM((T, T), bf16),
+                VMEM((3, F // 2, T), bf16),
                 VMEM((N, SEG, D), bf16),
                 dma((4,)),
                 dma((Y + 1, CHUNKS)),

time: 122 us -> 122 us (level)
  no operation moved by 1% of the time
where the time goes in v4:
time: 122 us
  Pallas kernels  119 us (98%)
  local copies, waits for them, and re-layouts  1.87 us (2%)
    pallas_call x1, Pallas kernels, per_device(): pl.pallas_call(functools.partial(layer_kernel, Y, Z, H, UP, DOWN, window)...  119 us

profile of v4, /device:TPU:1, one launch (start us, length us, event | category | flops | bytes accessed | tf_op | source)
XLA Modules:
  0.0 122.0 jit_solution(2222390441569958086)
XLA Ops:
  0.7 119.4 %ttt_layer.1 = bf16[64,8,512]{2,1,0:T(8,128)(2,1)} custom-call(bf16[512,512]{1,0:T(8,128)(2,1)} %bitcast.10, bf16[512,512]{1,0:T(8,128)(2,1)} %bitcast.11, bf16[512,512]{1,0:T(8,128)(2,1)} %bitcast.12, bf16[3,512,512]{2,1,0:T(8,128)(2,1)} %bitcast.9, f32[1]{0:T(128)S(6)} %copy.10.lr_ref, f32[1,512]{1,0:T(1,128)} %gain_ref.1, s32[2]{0:T(128)} %len_ref.1, ...), custom_call_target="tpu_custom_call" | custom-call | tf_op jit(solution)/shard_map/ttt_layer/pallas_call | solution.py:517
  120.1 1.9 %copy.11 = bf16[512,1,512]{2,0,1:T(8,128)(2,1)} copy(bf16[512,1,512]{2,0,1:T(8,128)(2,1)} %bitcast.8) | data formatting | bytes 1048576
